TPU v7x, 128 devices: a whole 4x4x4 slice. The times are simulated.
128 devices in a mesh: trow: 4 (over x_lo, core), tcol: 4 (over z), visit: 8 (over x_hi, y).
Axes of the slice: x: 4 (x_hi: 2, x_lo: 2; x = x_hi * 2 + x_lo), y: 4, z: 4, core: 2. Of those that a mesh axis runs over, the one named last changes fastest.
Arguments:
- template: float32 [2048, 2048], P(('trow', 'visit'), 'tcol'), may hold values from -6 to 6
- warped: float32 [1536, 256, 256], P(('trow', 'tcol', 'visit')), may hold values from -6 to 6
- coeffs: float32 [1536, 27, 3], P(('trow', 'tcol', 'visit')), may hold values from -2 to 2
- dest_tile: int32 [1536, 1], P(('trow', 'tcol', 'visit')), may hold values from 0 to 15; in each aligned block of 12 rows (0 to 11, 12 to 23, ...) at most 2 rows name the same one
- position: int32 [1536, 1], P(('trow', 'tcol', 'visit')), may hold values from 0 to 3
Outputs:
- difference: float32 [1536, 256, 256], P(('trow', 'tcol', 'visit'))
Inputs may be any that keep to these rules, and one draw needn't show every extreme that they name: `dest_tile`: tile index = tract row times the number of tract columns plus tract column; among the 12 blocks of one device no tile is named more than 2 times. `position`: sub-block row times 512 / 256 plus sub-block column.
All inputs are finite; a program needn't handle non-finite values.
Results may differ from a plain program's by a relative error of at most 0.0003.
Values sent between devices are 32-bit elements; how exact they have to be, the bound alone decides.
No kernel may reach another device: no remote copies, remote signals or barrier semaphores. Data moves between devices by JAX's collectives and lax.ppermute only.
A program may use at most 192 MiB of HBM per device.

v0:
```python
import jax
import jax.numpy as jnp
import numpy as np
from jax import lax
from jax.experimental import pallas as pl
from jax.experimental.pallas import tpu as pltpu
from jax.sharding import PartitionSpec as P

BLK = 256
HALF = 10
SPREADS = (1.0, 2.0, 4.0)
DEGREES = (4, 2, 2)
FILTERS = [(s, k) for s, d in enumerate(DEGREES) for k in range(d + 1)]
NF = len(FILTERS)
BASIS = {}
for _s, _d in enumerate(DEGREES):
    for _i in range(_d + 1):
        for _j in range(_d + 1 - _i):
            BASIS[(_s, _i, _j)] = len(BASIS)
MAXI = max(DEGREES) + 1

M = 32
CH = M + 32
SPAN = 84
LANES = 768
NT = BLK // M
KK = NF * CH
WR = 288
WC = 512
ROFF = 16 - HALF
COFF = 128 - HALF


def taps_for(spread, power):
    offsets = np.arange(-HALF, HALF + 1).astype(np.float32)
    weights = np.exp(-offsets * offsets / np.float32(2.0 * spread * spread)).astype(np.float32)
    for _ in range(power):
        weights = weights * offsets
    return (weights / np.sqrt(np.sum(weights * weights))).astype(np.float32)


def column_filters():
    one = np.zeros((SPAN, 12, 64), np.float32)
    for f, (s, k) in enumerate(FILTERS):
        taps = taps_for(SPREADS[s], k)
        for y in range(64):
            one[y : y + 21, f, y] = taps
    two = one.reshape(SPAN, 6, 2, 64)[:, :, ::-1]
    both = np.stack([one.reshape(SPAN, LANES), two.reshape(SPAN, LANES)])
    high = both.astype(jnp.bfloat16)
    low = (both - high.astype(np.float32)).astype(jnp.bfloat16)
    out = np.zeros((2, 256, LANES), jnp.bfloat16)
    out[:, 0:SPAN], out[:, SPAN : 2 * SPAN], out[:, 2 * SPAN : 3 * SPAN] = high, high, low
    return out


def row_filters():
    out = np.zeros((MAXI, M, NF, CH), np.float32)
    for f, (s, k) in enumerate(FILTERS):
        for i in range(DEGREES[s] + 1 - k):
            taps = taps_for(SPREADS[s], i)
            for x in range(M):
                out[i, x, f, x + ROFF : x + ROFF + 21] = taps
    return out.reshape(MAXI, M, KK)


def split(value):
    high = value.astype(jnp.bfloat16)
    low = (value - high.astype(jnp.float32)).astype(jnp.bfloat16)
    return high, low


def mix_kernel(coef_ref, rows_ref, flat_ref, slope_ref):
    def mixed(g):
        total = coef_ref[0, g, 0:1, :] * rows_ref[0]
        for i in range(1, MAXI):
            total = total + coef_ref[0, g, i : i + 1, :] * rows_ref[i]
        return total

    const, across, down = mixed(0), mixed(1), mixed(2)
    high, low = split(across)
    slope_ref[0, 0:M, :] = high
    slope_ref[0, M : 2 * M, :] = low
    half = (BLK - 1) / 2.0
    for t in range(NT):
        row = lax.broadcasted_iota(jnp.int32, (M, 1), 0) + t * M
        weight = (row.astype(jnp.float32) - half) * (1.0 / half)
        high, low = split(const + weight * down)
        flat_ref[0, t, 0:M, :] = high
        flat_ref[0, t, M : 2 * M, :] = low


def coefficient_rows(coeffs):
    index = np.zeros((MAXI, NF), np.int32)
    valid = np.zeros((MAXI, NF), np.float32)
    for f, (s, k) in enumerate(FILTERS):
        for i in range(DEGREES[s] + 1 - k):
            index[i, f] = BASIS[(s, i, k)]
            valid[i, f] = 1.0
    picked = jnp.stack(
        [jnp.stack([coeffs[:, int(index[i, f]), :] * float(valid[i, f]) for f in range(NF)], 1) for i in range(MAXI)], 1
    )
    return jnp.repeat(jnp.transpose(picked, (0, 3, 1, 2)), CH, axis=3)


def mix_rows(lanes):
    nb = lanes.shape[0]
    return pl.pallas_call(
        mix_kernel,
        grid=(nb,),
        in_specs=[
            pl.BlockSpec((1, 3, MAXI, KK), lambda b: (b, 0, 0, 0)),
            pl.BlockSpec((MAXI, M, KK), lambda b: (0, 0, 0)),
        ],
        out_specs=[
            pl.BlockSpec((1, NT, 2 * M, KK), lambda b: (b, 0, 0, 0)),
            pl.BlockSpec((1, 2 * M, KK), lambda b: (b, 0, 0)),
        ],
        out_shape=[
            jax.ShapeDtypeStruct((nb, NT, 2 * M, KK), jnp.bfloat16),
            jax.ShapeDtypeStruct((nb, 2 * M, KK), jnp.bfloat16),
        ],
        name="mix_rows",
        cost_estimate=pl.CostEstimate(flops=10**8, bytes_accessed=2 * 10**7, transcendentals=0),
    )(lanes, jnp.asarray(row_filters()))


def model_kernel(index_ref, line_ref, *refs):
    pieces = refs[:PIECES]
    warped_ref, flat_ref, slope_ref, cols_ref, out_ref, image, packed, vh, vl, sem = refs[PIECES:]
    n = pl.program_id(0)

    @pl.when(n == 0)
    def _():
        copies = []
        for p, (start, size) in enumerate(PLACES):
            copies.append(pltpu.make_async_copy(pieces[p], image.at[pl.ds(start, size)], sem.at[p]))
        for copy in copies:
            copy.start()
        for copy in copies:
            copy.wait()

    q, h, my_y = line_ref[3 * n], line_ref[3 * n + 1], line_ref[3 * n + 2]
    strips = [(0, 3, 48, 16, q > 0)] + [(1, k, 0, 64, None) for k in range(4)] + [(2, 0, 0, 16, q < 7)]
    lane = lax.broadcasted_iota(jnp.int32, (64, 128), 1)
    at = 0
    for a, k, first, height, inside in strips:
        d = lax.rem(k - my_y + 4, 4)
        rows = pl.ds(first, height)
        left = image[index_ref[n * 9 + 3 * a], d, rows, 128:256]
        body = image[index_ref[n * 9 + 3 * a + 1], d, rows, :]
        right = image[index_ref[n * 9 + 3 * a + 2], d, rows, 0:128]
        left = jnp.where(h > 0, left, 0.0)
        right = jnp.where(h < 7, right, 0.0)
        wide = jnp.concatenate([left, body, right], axis=1)
        if inside is not None:
            wide = jnp.where(inside, wide, 0.0)
        where = lane[0:height]
        for t in range(4):
            moved = pltpu.roll(wide, WC - COFF - 64 * (t % 2), axis=1)
            value = moved[:, 128 * (t // 2) : 128 * (t // 2) + 128]
            high = value.astype(jnp.bfloat16).astype(jnp.float32)
            low = pltpu.roll(value - high, SPAN, axis=1)
            again = pltpu.roll(high, 2 * SPAN - 128, axis=1)
            packed[t, at : at + height, :] = jnp.concatenate(
                [jnp.where(where < SPAN, high, low), jnp.where(where < 2 * SPAN - 128, low, again)], axis=1
            ).astype(jnp.bfloat16)
        at += height

    lane = lax.broadcasted_iota(jnp.int32, (WR, 128), 1)
    for g in range(3):
        lanes = slice(256 * g, 256 * g + 256)
        passed = [jnp.dot(packed[t], cols_ref[t % 2, :, lanes], preferred_element_type=jnp.float32) for t in range(4)]
        for p in range(2):
            f = 4 * g + 2 * p
            cut = [value[:, 128 * p : 128 * p + 128] for value in passed]
            straight = [jnp.where(lane < 64, cut[0], cut[1]), jnp.where(lane < 64, cut[2], cut[3])]
            vh[f], vl[f] = split(jnp.concatenate(straight, axis=1))
            if f + 1 < NF:
                swapped = [jnp.where(lane < 64, cut[1], cut[0]), jnp.where(lane < 64, cut[3], cut[2])]
                vh[f + 1], vl[f + 1] = split(jnp.concatenate([pltpu.roll(v, 64, axis=1) for v in swapped], axis=1))

    mid = (BLK - 1) / 2.0
    across = (lax.broadcasted_iota(jnp.int32, (1, BLK), 1).astype(jnp.float32) - mid) * (1.0 / mid)
    for t in range(NT):
        start = t * M
        wh = vh[:, start : start + CH, :].reshape(KK, BLK)
        wl = vl[:, start : start + CH, :].reshape(KK, BLK)
        lhs = jnp.concatenate([flat_ref[0, t, 0:M], slope_ref[0, 0:M], flat_ref[0, t, M : 2 * M], slope_ref[0, M : 2 * M]], axis=0)
        first = jnp.dot(lhs, wh, preferred_element_type=jnp.float32)
        second = jnp.dot(lhs[0 : 2 * M], wl, preferred_element_type=jnp.float32)
        flat = first[0:M] + first[2 * M : 3 * M] + second[0:M]
        slope = first[M : 2 * M] + first[3 * M : 4 * M] + second[M : 2 * M]
        out_ref[0, start : start + M, :] = warped_ref[0, start : start + M, :] - (flat + across * slope)


def difference(pieces, warped, rows, index, line):
    nb = warped.shape[0]
    spec = pltpu.PrefetchScalarGridSpec(
        num_scalar_prefetch=2,
        grid=(nb,),
        in_specs=[pl.BlockSpec(memory_space=pl.ANY)] * PIECES
        + [
            pl.BlockSpec((1, BLK, BLK), lambda b, *_: (b, 0, 0)),
            pl.BlockSpec((1, NT, 2 * M, KK), lambda b, *_: (b, 0, 0, 0)),
            pl.BlockSpec((1, 2 * M, KK), lambda b, *_: (b, 0, 0)),
            pl.BlockSpec((2, 256, LANES), lambda b, *_: (0, 0, 0)),
        ],
        out_specs=pl.BlockSpec((1, BLK, BLK), lambda b, *_: (b, 0, 0)),
        scratch_shapes=[
            pltpu.VMEM((64, 4, 64, BLK), jnp.float32),
            pltpu.VMEM((4, WR, 256), jnp.bfloat16),
            pltpu.VMEM((NF, WR, BLK), jnp.bfloat16),
            pltpu.VMEM((NF, WR, BLK), jnp.bfloat16),
            pltpu.SemaphoreType.DMA((PIECES,)),
        ],
    )
    return pl.pallas_call(
        model_kernel,
        grid_spec=spec,
        out_shape=jax.ShapeDtypeStruct((nb, BLK, BLK), jnp.float32),
        name="difference",
        compiler_params=pltpu.CompilerParams(vmem_limit_bytes=36 * 2**20),
    )(index, line, *pieces, warped, *rows, jnp.asarray(column_filters()))


AXES = ("trow", "tcol", "visit")


def device_of(x, y, z, core):
    return ((x % 2 * 2 + core) * 4 + z) * 8 + x // 2 * 4 + y


def fetch(value, x=0, y=0, z=0, core=0):
    pairs = []
    for i in range(4):
        for j in range(4):
            for k in range(4):
                for c in range(2):
                    source = device_of((i + x) % 4, (j + y) % 4, (k + z) % 4, (c + core) % 2)
                    pairs.append((source, device_of(i, j, k, c)))
    return lax.ppermute(value, AXES, pairs)


def ring(value, axis):
    return [value] + [fetch(value, **{axis: d}) for d in (1, 2, 3)]


PLACES = [(((half * 4 + ds) * 2 + dc) * 4 + d1, 2) for half in range(2) for ds in range(4) for dc in range(2) for d1 in (0, 2)]
PIECES = len(PLACES)


def gather_template(template, lanes, lines):
    strips, lanes = lax.optimization_barrier((jnp.stack(ring(template, "y")), lanes))
    halves, parts = [], []
    for half, (first, second) in enumerate((("x", "z"), ("z", "x"))):
        square = ring(strips[:, :, half * BLK : (half + 1) * BLK], first)
        a, b = jnp.stack(square[:2]), jnp.stack(square[2:])
        near_a = fetch(a, **{second: 1})
        last_b = fetch(b, **{second: 3})
        near_b = fetch(b, **{second: 1})
        last_a = fetch(a, **{second: 3})
        halves.append([a, b, near_a, near_b, last_a, last_b])
    rows = mix_rows(lanes)
    halves[0][2], rows, lines = lax.optimization_barrier((halves[0][2], rows, lines))
    for half, second in enumerate(("z", "x")):
        a, b, near_a, near_b, last_a, last_b = halves[half]
        far_a = fetch(near_a, **{second: 1})
        far_b = fetch(last_b, **{second: 3})
        for pair in ((a, b), (near_a, near_b), (far_a, far_b), (last_a, last_b)):
            parts.extend(pair)
            for p in pair:
                parts.append(fetch(p, core=1))
    return parts, lines, rows


def sub_index(q, h):
    trow, visit = lax.axis_index("trow"), lax.axis_index("visit")
    my_x, my_z, my_core = visit // 4 * 2 + trow // 2, lax.axis_index("tcol"), trow % 2
    tile_row, tile_col = q // 2, h // 2
    dx = (q % 2 * 2 + tile_row // 2 - my_x + 4) % 4
    dz = (tile_col - my_z + 4) % 4
    dc = (tile_row % 2 - my_core + 2) % 2
    by_z = (dz * 2 + dc) * 4 + dx
    by_x = 32 + (dx * 2 + dc) * 4 + dz
    return jnp.where(h % 2 == 0, by_z, by_x)


def window_index(dest_tile, position):
    q = dest_tile // 4 * 2 + position // 2
    h = dest_tile % 4 * 2 + position % 2
    near = jnp.array([-1, 0, 1], jnp.int32)
    rows = jnp.clip(q[:, None, None] + near[None, :, None], 0, 7)
    cols = jnp.clip(h[:, None, None] + near[None, None, :], 0, 7)
    index = sub_index(rows, cols).reshape(-1).astype(jnp.int32)
    my_y = jnp.broadcast_to(lax.axis_index("visit") % 4, q.shape)
    return index, jnp.stack([q, h, my_y], axis=1).reshape(-1).astype(jnp.int32)


def on_device(template, warped, coeffs, dest_tile, position):
    lines = window_index(dest_tile[:, 0], position[:, 0])
    pieces, (index, line), rows = gather_template(template, coefficient_rows(coeffs), lines)
    return difference(pieces, warped, rows, index, line)


def solution(mesh):
    return jax.shard_map(
        on_device,
        mesh=mesh,
        in_specs=(
            P(("trow", "visit"), "tcol"),
            P(("trow", "tcol", "visit"), None, None),
            P(("trow", "tcol", "visit"), None, None),
            P(("trow", "tcol", "visit"), None),
            P(("trow", "tcol", "visit"), None),
        ),
        out_specs=P(("trow", "tcol", "visit"), None, None),
        check_vma=False,
    )
```

profile of v0, /device:TPU:1, one launch (start us, length us, event | category | flops | bytes accessed | tf_op | source)
XLA Modules:
  0.0 150.8 jit_solution(4713477021684850084)
XLA Ops:
  0.0 3.6 %collective-permute-start = (f32[64,512]{1,0:T(8,128)}, f32[64,512]{1,0:T(8,128)S(1)}, u32[]{:S(2)}, u32[]{:S(2)}) collective-permute-start(f32[64,512]{1,0:T(8,128)} %param.8), channel_id=1, source_target_pairs={{1,0},{33,32},{9,8},{41,40},{17,16},{49,48},{25,24},{57,56},{2,1},... | collective-permute-start | bytes 393224 | tf_op jit(solution)/shard_map/ppermute | solution.py:242
  3.6 1.6 %collective-permute-start.1 = (f32[64,512]{1,0:T(8,128)}, f32[64,512]{1,0:T(8,128)S(1)}, u32[]{:S(2)}, u32[]{:S(2)}) collective-permute-start(f32[64,512]{1,0:T(8,128)} %param.8), channel_id=1, source_target_pairs={{2,0},{34,32},{10,8},{42,40},{18,16},{50,48},{26,24},{58,56},{3,1}... | collective-permute-start | bytes 393224 | tf_op jit(solution)/shard_map/ppermute | solution.py:242
  12.6 2.8 %collective-permute-start.5 = (f32[4,64,256]{2,1,0:T(8,128)S(1)}, f32[4,64,256]{2,1,0:T(8,128)S(1)}, u32[]{:S(2)}, u32[]{:S(2)}) collective-permute-start(f32[4,64,256]{2,1,0:T(8,128)S(1)} %get-tuple-element.26), channel_id=1, source_target_pairs={{4,0},{36,32},{12,8},{44,40},{20,16},{52,48},{28,24},{60,56},{5,1}... | collective-permute-start | bytes 786440 | tf_op jit(solution)/shard_map/ppermute | solution.py:242
  15.7 3.6 %collective-permute-start.21 = (f32[4,64,256]{2,1,0:T(8,128)S(1)}, f32[4,64,256]{2,1,0:T(8,128)S(1)}, u32[]{:S(2)}, u32[]{:S(2)}) collective-permute-start(f32[4,64,256]{2,1,0:T(8,128)S(1)} %get-tuple-element.25), channel_id=1, source_target_pairs={{16,0},{48,32},{24,8},{56,40},{0,16},{32,48},{8,24},{40,56},{17,1}... | collective-permute-start | bytes 786440 | tf_op jit(solution)/shard_map/ppermute | solution.py:242
  19.3 2.4 %collective-permute-start.3 = (f32[4,64,256]{2,1,0:T(8,128)S(1)}, f32[4,64,256]{2,1,0:T(8,128)S(1)}, u32[]{:S(2)}, u32[]{:S(2)}) collective-permute-start(f32[4,64,256]{2,1,0:T(8,128)S(1)} %get-tuple-element.26), channel_id=1, source_target_pairs={{64,0},{96,32},{72,8},{104,40},{80,16},{112,48},{88,24},{120,56},{... | collective-permute-start | bytes 786440 | tf_op jit(solution)/shard_map/ppermute | solution.py:242
  21.7 5.9 %collective-permute-done.6 = f32[4,64,256]{2,1,0:T(8,128)S(1)} collective-permute-done((f32[4,64,256]{2,1,0:T(8,128)S(1)}, f32[4,64,256]{2,1,0:T(8,128)S(1)}, u32[]{:S(2)}, u32[]{:S(2)}) %collective-permute-start.6) | collective-permute-done | bytes 262176 | tf_op jit(solution)/shard_map/ppermute | solution.py:242
  27.6 1.7 %collective-permute-start.13 = (f32[2,4,64,256]{3,2,1,0:T(8,128)S(1)}, f32[2,4,64,256]{3,2,1,0:T(8,128)S(1)}, u32[]{:S(2)}, u32[]{:S(2)}) collective-permute-start(f32[2,4,64,256]{3,2,1,0:T(8,128)S(1)} %pad_maximum_fusion.2.refs_1_), channel_id=1, source_target_pairs={{24,0},{56,32},{0,8},{32,40},{8,16},{40,48},{16,24},{48,56},{25,1}... | collective-permute-start | bytes 1572872 | tf_op jit(solution)/shard_map/ppermute | solution.py:242
  29.3 2.2 %collective-permute-start.9 = (f32[2,4,64,256]{3,2,1,0:T(8,128)S(1)}, f32[2,4,64,256]{3,2,1,0:T(8,128)S(1)}, u32[]{:S(2)}, u32[]{:S(2)}) collective-permute-start(f32[2,4,64,256]{3,2,1,0:T(8,128)S(1)} %pad_maximum_fusion.2.refs_1_), channel_id=1, source_target_pairs={{8,0},{40,32},{16,8},{48,40},{24,16},{56,48},{0,24},{32,56},{9,1},... | collective-permute-start | bytes 1572872 | tf_op jit(solution)/shard_map/ppermute | solution.py:242
  32.7 2.7 %collective-permute-start.20 = (f32[4,64,256]{2,1,0:T(8,128)S(1)}, f32[4,64,256]{2,1,0:T(8,128)S(1)}, u32[]{:S(2)}, u32[]{:S(2)}) collective-permute-start(f32[4,64,256]{2,1,0:T(8,128)S(1)} %get-tuple-element.25), channel_id=1, source_target_pairs={{8,0},{40,32},{16,8},{48,40},{24,16},{56,48},{0,24},{32,56},{9,1},... | collective-permute-start | bytes 786440 | tf_op jit(solution)/shard_map/ppermute | solution.py:242
  35.5 13.0 %collective-permute-done.22 = f32[4,64,256]{2,1,0:T(8,128)S(1)} collective-permute-done((f32[4,64,256]{2,1,0:T(8,128)S(1)}, f32[4,64,256]{2,1,0:T(8,128)S(1)}, u32[]{:S(2)}, u32[]{:S(2)}) %collective-permute-start.22) | collective-permute-done | bytes 262176 | tf_op jit(solution)/shard_map/ppermute | solution.py:242
  48.5 1.6 %collective-permute-start.7 = (f32[2,4,64,256]{3,2,1,0:T(8,128)S(1)}, f32[2,4,64,256]{3,2,1,0:T(8,128)S(1)}, u32[]{:S(2)}, u32[]{:S(2)}) collective-permute-start(f32[2,4,64,256]{3,2,1,0:T(8,128)S(1)} %pad_maximum_fusion.1.refs_0_), channel_id=1, source_target_pairs={{32,0},{0,32},{40,8},{8,40},{48,16},{16,48},{56,24},{24,56},{33,1}... | collective-permute-start | bytes 1572872 | tf_op jit(solution)/shard_map/ppermute | solution.py:242
  50.1 3.0 %collective-permute-start.4 = (f32[2,4,64,256]{3,2,1,0:T(8,128)S(1)}, f32[2,4,64,256]{3,2,1,0:T(8,128)S(1)}, u32[]{:S(2)}, u32[]{:S(2)}) collective-permute-start(f32[2,4,64,256]{3,2,1,0:T(8,128)S(1)} %pad_maximum_fusion.1.refs_0_), channel_id=1, source_target_pairs={{8,0},{40,32},{16,8},{48,40},{24,16},{56,48},{0,24},{32,56},{9,1},... | collective-permute-start | bytes 1572872 | tf_op jit(solution)/shard_map/ppermute | solution.py:242
  53.1 2.7 %collective-permute-start.26 = (f32[2,4,64,256]{3,2,1,0:T(8,128)S(1)}, f32[2,4,64,256]{3,2,1,0:T(8,128)S(1)}, u32[]{:S(2)}, u32[]{:S(2)}) collective-permute-start(f32[2,4,64,256]{3,2,1,0:T(8,128)S(1)} %pad_maximum_fusion.4.refs_17_), channel_id=1, source_target_pairs={{64,0},{96,32},{72,8},{104,40},{80,16},{112,48},{88,24},{120,56},{... | collective-permute-start | bytes 1572872 | tf_op jit(solution)/shard_map/ppermute | solution.py:242
  55.8 5.9 %collective-permute-done.17.refs_12_ = f32[2,4,64,256]{3,2,1,0:T(8,128)S(1)} collective-permute-done((f32[2,4,64,256]{3,2,1,0:T(8,128)S(1)}, f32[2,4,64,256]{3,2,1,0:T(8,128)S(1)}, u32[]{:S(2)}, u32[]{:S(2)}) %collective-permute-start.17) | collective-permute-done | bytes 524320 | tf_op jit(solution)/shard_map/ppermute | solution.py:242
  61.6 2.4 %collective-permute-start.24 = (f32[2,4,64,256]{3,2,1,0:T(8,128)S(1)}, f32[2,4,64,256]{3,2,1,0:T(8,128)}, u32[]{:S(2)}, u32[]{:S(2)}) collective-permute-start(f32[2,4,64,256]{3,2,1,0:T(8,128)S(1)} %pad_maximum_fusion.4.refs_17_), channel_id=1, source_target_pairs={{32,0},{0,32},{40,8},{8,40},{48,16},{16,48},{56,24},{24,56},{33,1}... | collective-permute-start | bytes 1572872 | tf_op jit(solution)/shard_map/ppermute | solution.py:242
  64.8 2.7 %collective-permute-start.25 = (f32[2,4,64,256]{3,2,1,0:T(8,128)S(1)}, f32[2,4,64,256]{3,2,1,0:T(8,128)}, u32[]{:S(2)}, u32[]{:S(2)}) collective-permute-start(f32[2,4,64,256]{3,2,1,0:T(8,128)S(1)} %pad_maximum_fusion.3.refs_16_), channel_id=1, source_target_pairs={{64,0},{96,32},{72,8},{104,40},{80,16},{112,48},{88,24},{120,56},{... | collective-permute-start | bytes 1572872 | tf_op jit(solution)/shard_map/ppermute | solution.py:242
  69.7 9.9 %collective-permute-done.34.refs_28_ = f32[2,4,64,256]{3,2,1,0:T(8,128)} collective-permute-done((f32[2,4,64,256]{3,2,1,0:T(8,128)S(1)}, f32[2,4,64,256]{3,2,1,0:T(8,128)}, u32[]{:S(2)}, u32[]{:S(2)}) %collective-permute-start.34) | collective-permute-done | bytes 524320 | tf_op jit(solution)/shard_map/ppermute | solution.py:242
  81.7 2.4 %copy.12.coef_ref = f32[12,3,5,704]{3,2,1,0:T(8,128)} copy(f32[12,3,5,704]{3,0,2,1:T(8,128)} %reshape.502) | data formatting | bytes 1013760 | tf_op jit(solution)/shard_map/optimization_barrier | solution.py:254
  84.1 9.9 %mix_rows.1 = (bf16[12,8,64,704]{3,2,1,0:T(8,128)(2,1)}, bf16[12,64,704]{2,1,0:T(8,128)(2,1)}) custom-call(f32[12,3,5,704]{3,2,1,0:T(8,128)} %copy.12.coef_ref, f32[5,32,704]{2,1,0:T(8,128)} %constant.169.clone.rows_ref), custom_call_target="tpu_custom_call" | custom-call | flops 100000000 | bytes 20000000 | tf_op jit(solution)/shard_map/mix_rows/pallas_call | solution.py:108
  94.5 2.6 %collective-permute-start.29 = (f32[2,4,64,256]{3,2,1,0:T(8,128)}, f32[2,4,64,256]{3,2,1,0:T(8,128)S(1)}, u32[]{:S(2)}, u32[]{:S(2)}) collective-permute-start(f32[2,4,64,256]{3,2,1,0:T(8,128)} %collective-permute-done.25.refs_20_), channel_id=1, source_target_pairs={{64,0},{96,32},{72,8},{104,40},{80,16},{112,48},{88,24},{120,56},{... | collective-permute-start | bytes 1572872 | tf_op jit(solution)/shard_map/ppermute | solution.py:242
  97.7 1.6 %collective-permute-start.12 = (f32[2,4,64,256]{3,2,1,0:T(8,128)}, f32[2,4,64,256]{3,2,1,0:T(8,128)S(1)}, u32[]{:S(2)}, u32[]{:S(2)}) collective-permute-start(f32[2,4,64,256]{3,2,1,0:T(8,128)} %copy-done.10), channel_id=1, source_target_pairs={{8,0},{40,32},{16,8},{48,40},{24,16},{56,48},{0,24},{32,56},{9,1},... | collective-permute-start | bytes 1572872 | tf_op jit(solution)/shard_map/ppermute | solution.py:242
  99.8 8.7 %collective-permute-done.29.refs_24_ = f32[2,4,64,256]{3,2,1,0:T(8,128)S(1)} collective-permute-done((f32[2,4,64,256]{3,2,1,0:T(8,128)}, f32[2,4,64,256]{3,2,1,0:T(8,128)S(1)}, u32[]{:S(2)}, u32[]{:S(2)}) %collective-permute-start.29) | collective-permute-done | bytes 524320 | tf_op jit(solution)/shard_map/ppermute | solution.py:242
  109.6 1.7 %collective-permute-done.12.refs_8_ = f32[2,4,64,256]{3,2,1,0:T(8,128)S(1)} collective-permute-done((f32[2,4,64,256]{3,2,1,0:T(8,128)}, f32[2,4,64,256]{3,2,1,0:T(8,128)S(1)}, u32[]{:S(2)}, u32[]{:S(2)}) %collective-permute-start.12) | collective-permute-done | bytes 524320 | tf_op jit(solution)/shard_map/ppermute | solution.py:242
  122.4 28.3 %difference.1 = f32[12,256,256]{2,1,0:T(8,128)} custom-call(s32[108]{0:T(128)S(1)} %select_n.202.index_ref, s32[36]{0:T(128)S(1)} %reshape.503.line_ref, f32[2,4,64,256]{3,2,1,0:T(8,128)S(1)} %pad_maximum_fusion.1.refs_0_, f32[2,4,64,256]{3,2,1,0:T(8,128)S(1)} %pad_maximum_fusion.2.refs_1_, f32[2,4,64,256]{3,2,1,0:T(8,128)S(1)} %copy-done.9, ...), custom_call_target="tpu_custom_call" | custom-call | tf_op jit(solution)/shard_map/difference/pallas_call | solution.py:218
  (125 shorter events, 27.6 us)
Async XLA Ops:
  15.7 17.0 %collective-permute-start.21 = (f32[4,64,256]{2,1,0:T(8,128)S(1)}, f32[4,64,256]{2,1,0:T(8,128)S(1)}, u32[]{:S(2)}, u32[]{:S(2)}) collective-permute-start(f32[4,64,256]{2,1,0:T(8,128)S(1)} %get-tuple-element.25), channel_id=1, source_target_pairs={{16,0},{48,32},{24,8},{56,40},{0,16},{32,48},{8,24},{40,56},{17,1}... | collective-permute-start | bytes 786440 | tf_op jit(solution)/shard_map/ppermute | solution.py:242
  19.3 13.4 %collective-permute-start.3 = (f32[4,64,256]{2,1,0:T(8,128)S(1)}, f32[4,64,256]{2,1,0:T(8,128)S(1)}, u32[]{:S(2)}, u32[]{:S(2)}) collective-permute-start(f32[4,64,256]{2,1,0:T(8,128)S(1)} %get-tuple-element.26), channel_id=1, source_target_pairs={{64,0},{96,32},{72,8},{104,40},{80,16},{112,48},{88,24},{120,56},{... | collective-permute-start | bytes 786440 | tf_op jit(solution)/shard_map/ppermute | solution.py:242
  27.6 22.5 %collective-permute-start.13 = (f32[2,4,64,256]{3,2,1,0:T(8,128)S(1)}, f32[2,4,64,256]{3,2,1,0:T(8,128)S(1)}, u32[]{:S(2)}, u32[]{:S(2)}) collective-permute-start(f32[2,4,64,256]{3,2,1,0:T(8,128)S(1)} %pad_maximum_fusion.2.refs_1_), channel_id=1, source_target_pairs={{24,0},{56,32},{0,8},{32,40},{8,16},{40,48},{16,24},{48,56},{25,1}... | collective-permute-start | bytes 1572872 | tf_op jit(solution)/shard_map/ppermute | solution.py:242
  29.3 23.7 %collective-permute-start.9 = (f32[2,4,64,256]{3,2,1,0:T(8,128)S(1)}, f32[2,4,64,256]{3,2,1,0:T(8,128)S(1)}, u32[]{:S(2)}, u32[]{:S(2)}) collective-permute-start(f32[2,4,64,256]{3,2,1,0:T(8,128)S(1)} %pad_maximum_fusion.2.refs_1_), channel_id=1, source_target_pairs={{8,0},{40,32},{16,8},{48,40},{24,16},{56,48},{0,24},{32,56},{9,1},... | collective-permute-start | bytes 1572872 | tf_op jit(solution)/shard_map/ppermute | solution.py:242
  31.5 21.5 %collective-permute-start.8 = (f32[2,4,64,256]{3,2,1,0:T(8,128)S(1)}, f32[2,4,64,256]{3,2,1,0:T(8,128)S(1)}, u32[]{:S(2)}, u32[]{:S(2)}) collective-permute-start(f32[2,4,64,256]{3,2,1,0:T(8,128)S(1)} %pad_maximum_fusion.2.refs_1_), channel_id=1, source_target_pairs={{32,0},{0,32},{40,8},{8,40},{48,16},{16,48},{56,24},{24,56},{33,1}... | collective-permute-start | bytes 1572872 | tf_op jit(solution)/shard_map/ppermute | solution.py:242
  32.7 15.7 %collective-permute-start.22 = (f32[4,64,256]{2,1,0:T(8,128)S(1)}, f32[4,64,256]{2,1,0:T(8,128)S(1)}, u32[]{:S(2)}, u32[]{:S(2)}) collective-permute-start(f32[4,64,256]{2,1,0:T(8,128)S(1)} %get-tuple-element.25), channel_id=1, source_target_pairs={{24,0},{56,32},{0,8},{32,40},{8,16},{40,48},{16,24},{48,56},{25,1}... | collective-permute-start | bytes 786440 | tf_op jit(solution)/shard_map/ppermute | solution.py:242
  32.7 15.7 %collective-permute-start.20 = (f32[4,64,256]{2,1,0:T(8,128)S(1)}, f32[4,64,256]{2,1,0:T(8,128)S(1)}, u32[]{:S(2)}, u32[]{:S(2)}) collective-permute-start(f32[4,64,256]{2,1,0:T(8,128)S(1)} %get-tuple-element.25), channel_id=1, source_target_pairs={{8,0},{40,32},{16,8},{48,40},{24,16},{56,48},{0,24},{32,56},{9,1},... | collective-permute-start | bytes 786440 | tf_op jit(solution)/shard_map/ppermute | solution.py:242
  48.4 13.2 %collective-permute-start.17 = (f32[2,4,64,256]{3,2,1,0:T(8,128)S(1)}, f32[2,4,64,256]{3,2,1,0:T(8,128)S(1)}, u32[]{:S(2)}, u32[]{:S(2)}) collective-permute-start(f32[2,4,64,256]{3,2,1,0:T(8,128)S(1)} %pad_maximum_fusion.1.refs_0_), channel_id=1, source_target_pairs={{24,0},{56,32},{0,8},{32,40},{8,16},{40,48},{16,24},{48,56},{25,1}... | collective-permute-start | bytes 1572872 | tf_op jit(solution)/shard_map/ppermute | solution.py:242
  48.5 15.5 %collective-permute-start.7 = (f32[2,4,64,256]{3,2,1,0:T(8,128)S(1)}, f32[2,4,64,256]{3,2,1,0:T(8,128)S(1)}, u32[]{:S(2)}, u32[]{:S(2)}) collective-permute-start(f32[2,4,64,256]{3,2,1,0:T(8,128)S(1)} %pad_maximum_fusion.1.refs_0_), channel_id=1, source_target_pairs={{32,0},{0,32},{40,8},{8,40},{48,16},{16,48},{56,24},{24,56},{33,1}... | collective-permute-start | bytes 1572872 | tf_op jit(solution)/shard_map/ppermute | solution.py:242
  50.1 14.7 %collective-permute-start.4 = (f32[2,4,64,256]{3,2,1,0:T(8,128)S(1)}, f32[2,4,64,256]{3,2,1,0:T(8,128)S(1)}, u32[]{:S(2)}, u32[]{:S(2)}) collective-permute-start(f32[2,4,64,256]{3,2,1,0:T(8,128)S(1)} %pad_maximum_fusion.1.refs_0_), channel_id=1, source_target_pairs={{8,0},{40,32},{16,8},{48,40},{24,16},{56,48},{0,24},{32,56},{9,1},... | collective-permute-start | bytes 1572872 | tf_op jit(solution)/shard_map/ppermute | solution.py:242
  53.0 14.5 %collective-permute-start.30 = (f32[2,4,64,256]{3,2,1,0:T(8,128)S(1)}, f32[2,4,64,256]{3,2,1,0:T(8,128)S(1)}, u32[]{:S(2)}, u32[]{:S(2)}) collective-permute-start(f32[2,4,64,256]{3,2,1,0:T(8,128)S(1)} %pad_maximum_fusion.4.refs_17_), channel_id=1, source_target_pairs={{68,0},{100,32},{76,8},{108,40},{84,16},{116,48},{92,24},{124,56},... | collective-permute-start | bytes 1572872 | tf_op jit(solution)/shard_map/ppermute | solution.py:242
  53.1 15.5 %collective-permute-start.26 = (f32[2,4,64,256]{3,2,1,0:T(8,128)S(1)}, f32[2,4,64,256]{3,2,1,0:T(8,128)S(1)}, u32[]{:S(2)}, u32[]{:S(2)}) collective-permute-start(f32[2,4,64,256]{3,2,1,0:T(8,128)S(1)} %pad_maximum_fusion.4.refs_17_), channel_id=1, source_target_pairs={{64,0},{96,32},{72,8},{104,40},{80,16},{112,48},{88,24},{120,56},{... | collective-permute-start | bytes 1572872 | tf_op jit(solution)/shard_map/ppermute | solution.py:242
  64.8 14.8 %collective-permute-start.34 = (f32[2,4,64,256]{3,2,1,0:T(8,128)S(1)}, f32[2,4,64,256]{3,2,1,0:T(8,128)}, u32[]{:S(2)}, u32[]{:S(2)}) collective-permute-start(f32[2,4,64,256]{3,2,1,0:T(8,128)S(1)} %pad_maximum_fusion.3.refs_16_), channel_id=1, source_target_pairs={{68,0},{100,32},{76,8},{108,40},{84,16},{116,48},{92,24},{124,56},... | collective-permute-start | bytes 1572872 | tf_op jit(solution)/shard_map/ppermute | solution.py:242
  64.8 15.6 %collective-permute-start.25 = (f32[2,4,64,256]{3,2,1,0:T(8,128)S(1)}, f32[2,4,64,256]{3,2,1,0:T(8,128)}, u32[]{:S(2)}, u32[]{:S(2)}) collective-permute-start(f32[2,4,64,256]{3,2,1,0:T(8,128)S(1)} %pad_maximum_fusion.3.refs_16_), channel_id=1, source_target_pairs={{64,0},{96,32},{72,8},{104,40},{80,16},{112,48},{88,24},{120,56},{... | collective-permute-start | bytes 1572872 | tf_op jit(solution)/shard_map/ppermute | solution.py:242
  67.5 13.0 %collective-permute-start.23 = (f32[2,4,64,256]{3,2,1,0:T(8,128)S(1)}, f32[2,4,64,256]{3,2,1,0:T(8,128)}, u32[]{:S(2)}, u32[]{:S(2)}) collective-permute-start(f32[2,4,64,256]{3,2,1,0:T(8,128)S(1)} %pad_maximum_fusion.3.refs_16_), channel_id=1, source_target_pairs={{32,0},{0,32},{40,8},{8,40},{48,16},{16,48},{56,24},{24,56},{33,1}... | collective-permute-start | bytes 1572872 | tf_op jit(solution)/shard_map/ppermute | solution.py:242
  69.6 24.4 %collective-permute-start.14 = (f32[2,4,64,256]{3,2,1,0:T(8,128)S(1)}, f32[2,4,64,256]{3,2,1,0:T(8,128)}, u32[]{:S(2)}, u32[]{:S(2)}) collective-permute-start(f32[2,4,64,256]{3,2,1,0:T(8,128)S(1)} %collective-permute-done.13.refs_13_), channel_id=1, source_target_pairs={{24,0},{56,32},{0,8},{32,40},{8,16},{40,48},{16,24},{48,56},{25,1}... | collective-permute-start | bytes 1572872 | tf_op jit(solution)/shard_map/ppermute | solution.py:242
  79.6 17.6 %collective-permute-start.36 = (f32[2,4,64,256]{3,2,1,0:T(8,128)}, f32[2,4,64,256]{3,2,1,0:T(8,128)}, u32[]{:S(2)}, u32[]{:S(2)}) collective-permute-start(f32[2,4,64,256]{3,2,1,0:T(8,128)} %copy-done.12), channel_id=1, source_target_pairs={{32,0},{0,32},{40,8},{8,40},{48,16},{16,48},{56,24},{24,56},{33,1}... | collective-permute-start | bytes 1572872 | tf_op jit(solution)/shard_map/ppermute | solution.py:242
  80.5 17.2 %collective-permute-start.31 = (f32[2,4,64,256]{3,2,1,0:T(8,128)}, f32[2,4,64,256]{3,2,1,0:T(8,128)}, u32[]{:S(2)}, u32[]{:S(2)}) collective-permute-start(f32[2,4,64,256]{3,2,1,0:T(8,128)} %copy-done.12), channel_id=1, source_target_pairs={{68,0},{100,32},{76,8},{108,40},{84,16},{116,48},{92,24},{124,56},... | collective-permute-start | bytes 1572872 | tf_op jit(solution)/shard_map/ppermute | solution.py:242
  80.5 13.8 %collective-permute-start.11 = (f32[2,4,64,256]{3,2,1,0:T(8,128)}, f32[2,4,64,256]{3,2,1,0:T(8,128)}, u32[]{:S(2)}, u32[]{:S(2)}) collective-permute-start(f32[2,4,64,256]{3,2,1,0:T(8,128)} %copy-done.2), channel_id=1, source_target_pairs={{32,0},{0,32},{40,8},{8,40},{48,16},{16,48},{56,24},{24,56},{33,1}... | collective-permute-start | bytes 1572872 | tf_op jit(solution)/shard_map/ppermute | solution.py:242
  80.6 13.9 %collective-permute-start.18 = (f32[2,4,64,256]{3,2,1,0:T(8,128)}, f32[2,4,64,256]{3,2,1,0:T(8,128)}, u32[]{:S(2)}, u32[]{:S(2)}) collective-permute-start(f32[2,4,64,256]{3,2,1,0:T(8,128)} %copy-done.6), channel_id=1, source_target_pairs={{32,0},{0,32},{40,8},{8,40},{48,16},{16,48},{56,24},{24,56},{33,1}... | collective-permute-start | bytes 1572872 | tf_op jit(solution)/shard_map/ppermute | solution.py:242
  94.5 14.0 %collective-permute-start.29 = (f32[2,4,64,256]{3,2,1,0:T(8,128)}, f32[2,4,64,256]{3,2,1,0:T(8,128)S(1)}, u32[]{:S(2)}, u32[]{:S(2)}) collective-permute-start(f32[2,4,64,256]{3,2,1,0:T(8,128)} %collective-permute-done.25.refs_20_), channel_id=1, source_target_pairs={{64,0},{96,32},{72,8},{104,40},{80,16},{112,48},{88,24},{120,56},{... | collective-permute-start | bytes 1572872 | tf_op jit(solution)/shard_map/ppermute | solution.py:242
  97.7 13.6 %collective-permute-start.12 = (f32[2,4,64,256]{3,2,1,0:T(8,128)}, f32[2,4,64,256]{3,2,1,0:T(8,128)S(1)}, u32[]{:S(2)}, u32[]{:S(2)}) collective-permute-start(f32[2,4,64,256]{3,2,1,0:T(8,128)} %copy-done.10), channel_id=1, source_target_pairs={{8,0},{40,32},{16,8},{48,40},{24,16},{56,48},{0,24},{32,56},{9,1},... | collective-permute-start | bytes 1572872 | tf_op jit(solution)/shard_map/ppermute | solution.py:242
  99.3 12.9 %collective-permute-start.10 = (f32[2,4,64,256]{3,2,1,0:T(8,128)}, f32[2,4,64,256]{3,2,1,0:T(8,128)S(1)}, u32[]{:S(2)}, u32[]{:S(2)}) collective-permute-start(f32[2,4,64,256]{3,2,1,0:T(8,128)} %copy-done.10), channel_id=1, source_target_pairs={{32,0},{0,32},{40,8},{8,40},{48,16},{16,48},{56,24},{24,56},{33,1}... | collective-permute-start | bytes 1572872 | tf_op jit(solution)/shard_map/ppermute | solution.py:242
  99.7 12.6 %collective-permute-start.16 = (f32[2,4,64,256]{3,2,1,0:T(8,128)}, f32[2,4,64,256]{3,2,1,0:T(8,128)S(1)}, u32[]{:S(2)}, u32[]{:S(2)}) collective-permute-start(f32[2,4,64,256]{3,2,1,0:T(8,128)} %collective-permute-done.14.refs_9_), channel_id=1, source_target_pairs={{32,0},{0,32},{40,8},{8,40},{48,16},{16,48},{56,24},{24,56},{33,1}... | collective-permute-start | bytes 1572872 | tf_op jit(solution)/shard_map/ppermute | solution.py:242
  (33 other events, 404.2 us)
where the time goes:
time: 152 us; the launch traced here: 151 us
  waiting for transfers between devices  46.6 us (31%)
  starting transfers between devices  44.9 us (30%)
  Pallas kernels  38.2 us (25%)
  local copies, waits for them, and re-layouts  18.2 us (12%)
  other arithmetic  2.39 us (2%)
    ppermute x37, waiting for transfers between devices, fetch(): return lax.ppermute(value, AXES, pairs)  46.6 us
    ppermute x37, starting transfers between devices, fetch(): return lax.ppermute(value, AXES, pairs)  44.9 us
    pallas_call x1, Pallas kernels, difference(): pl.pallas_call(model_kernel, grid_spec=spec, out_shape=jax.ShapeDtypeStru...  28.3 us
    unnamed x43, local copies, waits for them, and re-layouts  10.1 us
    pallas_call x1, Pallas kernels, mix_rows(): pl.pallas_call(mix_kernel, grid=(nb,), in_specs=[pl.BlockSpec((1, 3, MAXI...  9.94 us
  transfers between devices with their start and end apart: 37, of which 7 were waited for; matrix products, arithmetic and copies ran while one was open for 7% of the time, Pallas kernels for 7%

commit v1 on v0

--- a/solution.py
+++ b/solution.py
@@ -70,24 +70,29 @@
     return high, low
 
 
-def mix_kernel(coef_ref, rows_ref, flat_ref, slope_ref):
-    def mixed(g):
-        total = coef_ref[0, g, 0:1, :] * rows_ref[0]
-        for i in range(1, MAXI):
-            total = total + coef_ref[0, g, i : i + 1, :] * rows_ref[i]
-        return total
-
-    const, across, down = mixed(0), mixed(1), mixed(2)
-    high, low = split(across)
-    slope_ref[0, 0:M, :] = high
-    slope_ref[0, M : 2 * M, :] = low
+MIX = 2
+
+
+def mix_kernel(coef_ref, rows_ref, out_ref):
     half = (BLK - 1) / 2.0
-    for t in range(NT):
-        row = lax.broadcasted_iota(jnp.int32, (M, 1), 0) + t * M
-        weight = (row.astype(jnp.float32) - half) * (1.0 / half)
-        high, low = split(const + weight * down)
-        flat_ref[0, t, 0:M, :] = high
-        flat_ref[0, t, M : 2 * M, :] = low
+    for k in range(MIX):
+
+        def mixed(g):
+            total = coef_ref[k, 5 * g : 5 * g + 1, :] * rows_ref[0]
+            for i in range(1, MAXI):
+                total = total + coef_ref[k, 5 * g + i : 5 * g + i + 1, :] * rows_ref[i]
+            return total
+
+        const, across, down = mixed(0), mixed(1), mixed(2)
+        high, low = split(across)
+        out_ref[k, NT, 0:M, :] = high
+        out_ref[k, NT, M : 2 * M, :] = low
+        for t in range(NT):
+            row = lax.broadcasted_iota(jnp.int32, (M, 1), 0) + t * M
+            weight = (row.astype(jnp.float32) - half) * (1.0 / half)
+            high, low = split(const + weight * down)
+            out_ref[k, t, 0:M, :] = high
+            out_ref[k, t, M : 2 * M, :] = low
 
 
 def coefficient_rows(coeffs):
@@ -100,26 +105,22 @@
     picked = jnp.stack(
         [jnp.stack([coeffs[:, int(index[i, f]), :] * float(valid[i, f]) for f in range(NF)], 1) for i in range(MAXI)], 1
     )
-    return jnp.repeat(jnp.transpose(picked, (0, 3, 1, 2)), CH, axis=3)
+    table = jnp.transpose(picked, (0, 3, 1, 2)).reshape(-1, 3 * MAXI, NF)
+    table = jnp.pad(table, ((0, 0), (0, 1), (0, 0)))
+    return jnp.repeat(table, CH, axis=2)
 
 
 def mix_rows(lanes):
     nb = lanes.shape[0]
     return pl.pallas_call(
         mix_kernel,
-        grid=(nb,),
+        grid=(nb // MIX,),
         in_specs=[
-            pl.BlockSpec((1, 3, MAXI, KK), lambda b: (b, 0, 0, 0)),
+            pl.BlockSpec((MIX, 16, KK), lambda b: (b, 0, 0)),
             pl.BlockSpec((MAXI, M, KK), lambda b: (0, 0, 0)),
         ],
-        out_specs=[
-            pl.BlockSpec((1, NT, 2 * M, KK), lambda b: (b, 0, 0, 0)),
-            pl.BlockSpec((1, 2 * M, KK), lambda b: (b, 0, 0)),
-        ],
-        out_shape=[
-            jax.ShapeDtypeStruct((nb, NT, 2 * M, KK), jnp.bfloat16),
-            jax.ShapeDtypeStruct((nb, 2 * M, KK), jnp.bfloat16),
-        ],
+        out_specs=pl.BlockSpec((MIX, NT + 1, 2 * M, KK), lambda b: (b, 0, 0, 0)),
+        out_shape=jax.ShapeDtypeStruct((nb, NT + 1, 2 * M, KK), jnp.bfloat16),
         name="mix_rows",
         cost_estimate=pl.CostEstimate(flops=10**8, bytes_accessed=2 * 10**7, transcendentals=0),
     )(lanes, jnp.asarray(row_filters()))
@@ -127,7 +128,7 @@
 
 def model_kernel(index_ref, line_ref, *refs):
     pieces = refs[:PIECES]
-    warped_ref, flat_ref, slope_ref, cols_ref, out_ref, image, packed, vh, vl, sem = refs[PIECES:]
+    warped_ref, mix_ref, cols_ref, out_ref, image, packed, vh, vl, sem = refs[PIECES:]
     n = pl.program_id(0)
 
     @pl.when(n == 0)
@@ -186,7 +187,7 @@
         start = t * M
         wh = vh[:, start : start + CH, :].reshape(KK, BLK)
         wl = vl[:, start : start + CH, :].reshape(KK, BLK)
-        lhs = jnp.concatenate([flat_ref[0, t, 0:M], slope_ref[0, 0:M], flat_ref[0, t, M : 2 * M], slope_ref[0, M : 2 * M]], axis=0)
+        lhs = jnp.concatenate([mix_ref[0, t, 0:M], mix_ref[0, NT, 0:M], mix_ref[0, t, M : 2 * M], mix_ref[0, NT, M : 2 * M]], axis=0)
         first = jnp.dot(lhs, wh, preferred_element_type=jnp.float32)
         second = jnp.dot(lhs[0 : 2 * M], wl, preferred_element_type=jnp.float32)
         flat = first[0:M] + first[2 * M : 3 * M] + second[0:M]
@@ -202,8 +203,7 @@
         in_specs=[pl.BlockSpec(memory_space=pl.ANY)] * PIECES
         + [
             pl.BlockSpec((1, BLK, BLK), lambda b, *_: (b, 0, 0)),
-            pl.BlockSpec((1, NT, 2 * M, KK), lambda b, *_: (b, 0, 0, 0)),
-            pl.BlockSpec((1, 2 * M, KK), lambda b, *_: (b, 0, 0)),
+            pl.BlockSpec((1, NT + 1, 2 * M, KK), lambda b, *_: (b, 0, 0, 0)),
             pl.BlockSpec((2, 256, LANES), lambda b, *_: (0, 0, 0)),
         ],
         out_specs=pl.BlockSpec((1, BLK, BLK), lambda b, *_: (b, 0, 0)),
@@ -221,7 +221,7 @@
         out_shape=jax.ShapeDtypeStruct((nb, BLK, BLK), jnp.float32),
         name="difference",
         compiler_params=pltpu.CompilerParams(vmem_limit_bytes=36 * 2**20),
-    )(index, line, *pieces, warped, *rows, jnp.asarray(column_filters()))
+    )(index, line, *pieces, warped, rows, jnp.asarray(column_filters()))
 
 
 AXES = ("trow", "tcol", "visit")

time: 152 us -> 146 us (0.961)
  local copies, waits for them, and re-layouts: 18.2 us -> 14.1 us
  Pallas kernels: 38.2 us -> 36.2 us
    pallas_call x1, Pallas kernels: 9.94 us -> 7.56 us  [mix_rows(): pl.pallas_call(mix_kernel, grid=(nb // MIX,), in_specs=[pl.BlockSpec((MIX...]
    optimization_barrier x1 -> x0, local copies, waits for them, and re-layouts: 2.38 us -> none  [gather_template(): lax.optimization_barrier((jnp.stack(ring(template, 'y')), lanes))]
    unnamed x43 -> x35, local copies, waits for them, and re-layouts: 10.1 us -> 8.39 us
  transfers between devices with their start and end apart: 37 -> 37, of which waited for: 7 -> 8; matrix products, arithmetic and copies ran while one was open for 7% -> 6% of each run, Pallas kernels for 7% -> 5%
where the time goes in v1:
time: 146 us
  waiting for transfers between devices  47.8 us (33%)
  starting transfers between devices  44.7 us (31%)
  Pallas kernels  36.2 us (25%)
  local copies, waits for them, and re-layouts  14.1 us (10%)
  other arithmetic  2.39 us (2%)
    ppermute x37, waiting for transfers between devices, fetch(): return lax.ppermute(value, AXES, pairs)  47.8 us
    ppermute x37, starting transfers between devices, fetch(): return lax.ppermute(value, AXES, pairs)  44.7 us
    pallas_call x1, Pallas kernels, difference(): pl.pallas_call(model_kernel, grid_spec=spec, out_shape=jax.ShapeDtypeStru...  28.6 us
    unnamed x35, local copies, waits for them, and re-layouts  8.39 us
    pallas_call x1, Pallas kernels, mix_rows(): pl.pallas_call(mix_kernel, grid=(nb // MIX,), in_specs=[pl.BlockSpec((MIX...  7.56 us
  transfers between devices with their start and end apart: 37, of which 8 were waited for; matrix products, arithmetic and copies ran while one was open for 6% of the time, Pallas kernels for 5%

profile of v1, /device:TPU:1, one launch (start us, length us, event | category | flops | bytes accessed | tf_op | source)
XLA Modules:
  0.0 145.7 jit_solution(291717034765416283)
XLA Ops:
  0.0 3.6 %collective-permute-start = (f32[64,512]{1,0:T(8,128)}, f32[64,512]{1,0:T(8,128)S(1)}, u32[]{:S(2)}, u32[]{:S(2)}) collective-permute-start(f32[64,512]{1,0:T(8,128)} %param.8), channel_id=1, source_target_pairs={{1,0},{33,32},{9,8},{41,40},{17,16},{49,48},{25,24},{57,56},{2,1},... | collective-permute-start | bytes 393224 | tf_op jit(solution)/shard_map/ppermute | solution.py:242
  3.6 1.6 %collective-permute-start.1 = (f32[64,512]{1,0:T(8,128)}, f32[64,512]{1,0:T(8,128)S(1)}, u32[]{:S(2)}, u32[]{:S(2)}) collective-permute-start(f32[64,512]{1,0:T(8,128)} %param.8), channel_id=1, source_target_pairs={{2,0},{34,32},{10,8},{42,40},{18,16},{50,48},{26,24},{58,56},{3,1}... | collective-permute-start | bytes 393224 | tf_op jit(solution)/shard_map/ppermute | solution.py:242
  12.6 2.8 %collective-permute-start.5 = (f32[4,64,256]{2,1,0:T(8,128)S(1)}, f32[4,64,256]{2,1,0:T(8,128)S(1)}, u32[]{:S(2)}, u32[]{:S(2)}) collective-permute-start(f32[4,64,256]{2,1,0:T(8,128)S(1)} %get-tuple-element.20), channel_id=1, source_target_pairs={{4,0},{36,32},{12,8},{44,40},{20,16},{52,48},{28,24},{60,56},{5,1}... | collective-permute-start | bytes 786440 | tf_op jit(solution)/shard_map/ppermute | solution.py:242
  15.8 3.6 %collective-permute-start.21 = (f32[4,64,256]{2,1,0:T(8,128)S(1)}, f32[4,64,256]{2,1,0:T(8,128)S(1)}, u32[]{:S(2)}, u32[]{:S(2)}) collective-permute-start(f32[4,64,256]{2,1,0:T(8,128)S(1)} %get-tuple-element.19), channel_id=1, source_target_pairs={{16,0},{48,32},{24,8},{56,40},{0,16},{32,48},{8,24},{40,56},{17,1}... | collective-permute-start | bytes 786440 | tf_op jit(solution)/shard_map/ppermute | solution.py:242
  19.4 2.4 %collective-permute-start.3 = (f32[4,64,256]{2,1,0:T(8,128)S(1)}, f32[4,64,256]{2,1,0:T(8,128)S(1)}, u32[]{:S(2)}, u32[]{:S(2)}) collective-permute-start(f32[4,64,256]{2,1,0:T(8,128)S(1)} %get-tuple-element.20), channel_id=1, source_target_pairs={{64,0},{96,32},{72,8},{104,40},{80,16},{112,48},{88,24},{120,56},{... | collective-permute-start | bytes 786440 | tf_op jit(solution)/shard_map/ppermute | solution.py:242
  21.7 5.9 %collective-permute-done.6 = f32[4,64,256]{2,1,0:T(8,128)S(1)} collective-permute-done((f32[4,64,256]{2,1,0:T(8,128)S(1)}, f32[4,64,256]{2,1,0:T(8,128)S(1)}, u32[]{:S(2)}, u32[]{:S(2)}) %collective-permute-start.6) | collective-permute-done | bytes 262176 | tf_op jit(solution)/shard_map/ppermute | solution.py:242
  27.7 1.7 %collective-permute-start.13 = (f32[2,4,64,256]{3,2,1,0:T(8,128)S(1)}, f32[2,4,64,256]{3,2,1,0:T(8,128)S(1)}, u32[]{:S(2)}, u32[]{:S(2)}) collective-permute-start(f32[2,4,64,256]{3,2,1,0:T(8,128)S(1)} %pad_maximum_fusion.2.refs_1_), channel_id=1, source_target_pairs={{24,0},{56,32},{0,8},{32,40},{8,16},{40,48},{16,24},{48,56},{25,1}... | collective-permute-start | bytes 1572872 | tf_op jit(solution)/shard_map/ppermute | solution.py:242
  29.4 2.2 %collective-permute-start.9 = (f32[2,4,64,256]{3,2,1,0:T(8,128)S(1)}, f32[2,4,64,256]{3,2,1,0:T(8,128)}, u32[]{:S(2)}, u32[]{:S(2)}) collective-permute-start(f32[2,4,64,256]{3,2,1,0:T(8,128)S(1)} %pad_maximum_fusion.2.refs_1_), channel_id=1, source_target_pairs={{8,0},{40,32},{16,8},{48,40},{24,16},{56,48},{0,24},{32,56},{9,1},... | collective-permute-start | bytes 1572872 | tf_op jit(solution)/shard_map/ppermute | solution.py:242
  32.8 2.7 %collective-permute-start.20 = (f32[4,64,256]{2,1,0:T(8,128)S(1)}, f32[4,64,256]{2,1,0:T(8,128)S(1)}, u32[]{:S(2)}, u32[]{:S(2)}) collective-permute-start(f32[4,64,256]{2,1,0:T(8,128)S(1)} %get-tuple-element.19), channel_id=1, source_target_pairs={{8,0},{40,32},{16,8},{48,40},{24,16},{56,48},{0,24},{32,56},{9,1},... | collective-permute-start | bytes 786440 | tf_op jit(solution)/shard_map/ppermute | solution.py:242
  35.5 13.0 %collective-permute-done.22 = f32[4,64,256]{2,1,0:T(8,128)S(1)} collective-permute-done((f32[4,64,256]{2,1,0:T(8,128)S(1)}, f32[4,64,256]{2,1,0:T(8,128)S(1)}, u32[]{:S(2)}, u32[]{:S(2)}) %collective-permute-start.22) | collective-permute-done | bytes 262176 | tf_op jit(solution)/shard_map/ppermute | solution.py:242
  48.5 1.6 %collective-permute-start.7 = (f32[2,4,64,256]{3,2,1,0:T(8,128)S(1)}, f32[2,4,64,256]{3,2,1,0:T(8,128)S(1)}, u32[]{:S(2)}, u32[]{:S(2)}) collective-permute-start(f32[2,4,64,256]{3,2,1,0:T(8,128)S(1)} %pad_maximum_fusion.1.refs_0_), channel_id=1, source_target_pairs={{32,0},{0,32},{40,8},{8,40},{48,16},{16,48},{56,24},{24,56},{33,1}... | collective-permute-start | bytes 1572872 | tf_op jit(solution)/shard_map/ppermute | solution.py:242
  50.1 3.0 %collective-permute-start.4 = (f32[2,4,64,256]{3,2,1,0:T(8,128)S(1)}, f32[2,4,64,256]{3,2,1,0:T(8,128)S(1)}, u32[]{:S(2)}, u32[]{:S(2)}) collective-permute-start(f32[2,4,64,256]{3,2,1,0:T(8,128)S(1)} %pad_maximum_fusion.1.refs_0_), channel_id=1, source_target_pairs={{8,0},{40,32},{16,8},{48,40},{24,16},{56,48},{0,24},{32,56},{9,1},... | collective-permute-start | bytes 1572872 | tf_op jit(solution)/shard_map/ppermute | solution.py:242
  53.9 2.7 %collective-permute-start.26 = (f32[2,4,64,256]{3,2,1,0:T(8,128)S(1)}, f32[2,4,64,256]{3,2,1,0:T(8,128)S(1)}, u32[]{:S(2)}, u32[]{:S(2)}) collective-permute-start(f32[2,4,64,256]{3,2,1,0:T(8,128)S(1)} %pad_maximum_fusion.4.refs_17_), channel_id=1, source_target_pairs={{64,0},{96,32},{72,8},{104,40},{80,16},{112,48},{88,24},{120,56},{... | collective-permute-start | bytes 1572872 | tf_op jit(solution)/shard_map/ppermute | solution.py:242
  56.6 5.2 %collective-permute-done.17.refs_12_ = f32[2,4,64,256]{3,2,1,0:T(8,128)} collective-permute-done((f32[2,4,64,256]{3,2,1,0:T(8,128)S(1)}, f32[2,4,64,256]{3,2,1,0:T(8,128)}, u32[]{:S(2)}, u32[]{:S(2)}) %collective-permute-start.17) | collective-permute-done | bytes 524320 | tf_op jit(solution)/shard_map/ppermute | solution.py:242
  61.8 2.4 %collective-permute-start.24 = (f32[2,4,64,256]{3,2,1,0:T(8,128)S(1)}, f32[2,4,64,256]{3,2,1,0:T(8,128)S(1)}, u32[]{:S(2)}, u32[]{:S(2)}) collective-permute-start(f32[2,4,64,256]{3,2,1,0:T(8,128)S(1)} %pad_maximum_fusion.4.refs_17_), channel_id=1, source_target_pairs={{32,0},{0,32},{40,8},{8,40},{48,16},{16,48},{56,24},{24,56},{33,1}... | collective-permute-start | bytes 1572872 | tf_op jit(solution)/shard_map/ppermute | solution.py:242
  64.9 2.7 %collective-permute-start.25 = (f32[2,4,64,256]{3,2,1,0:T(8,128)S(1)}, f32[2,4,64,256]{3,2,1,0:T(8,128)}, u32[]{:S(2)}, u32[]{:S(2)}) collective-permute-start(f32[2,4,64,256]{3,2,1,0:T(8,128)S(1)} %pad_maximum_fusion.3.refs_16_), channel_id=1, source_target_pairs={{64,0},{96,32},{72,8},{104,40},{80,16},{112,48},{88,24},{120,56},{... | collective-permute-start | bytes 1572872 | tf_op jit(solution)/shard_map/ppermute | solution.py:242
  70.6 9.2 %collective-permute-done.34.refs_28_ = f32[2,4,64,256]{3,2,1,0:T(8,128)} collective-permute-done((f32[2,4,64,256]{3,2,1,0:T(8,128)S(1)}, f32[2,4,64,256]{3,2,1,0:T(8,128)}, u32[]{:S(2)}, u32[]{:S(2)}) %collective-permute-start.34) | collective-permute-done | bytes 524320 | tf_op jit(solution)/shard_map/ppermute | solution.py:242
  81.9 7.6 %mix_rows.1.refs_33_ = bf16[12,9,64,704]{3,2,1,0:T(8,128)(2,1)} custom-call(f32[12,16,704]{2,1,0:T(8,128)} %reshape.506.coef_ref, f32[5,32,704]{2,1,0:T(8,128)} %constant.170.clone.rows_ref), custom_call_target="tpu_custom_call" | custom-call | flops 100000000 | bytes 20000000 | tf_op jit(solution)/shard_map/mix_rows/pallas_call | solution.py:115
  89.9 2.6 %collective-permute-start.29 = (f32[2,4,64,256]{3,2,1,0:T(8,128)}, f32[2,4,64,256]{3,2,1,0:T(8,128)S(1)}, u32[]{:S(2)}, u32[]{:S(2)}) collective-permute-start(f32[2,4,64,256]{3,2,1,0:T(8,128)} %collective-permute-done.25.refs_20_), channel_id=1, source_target_pairs={{64,0},{96,32},{72,8},{104,40},{80,16},{112,48},{88,24},{120,56},{... | collective-permute-start | bytes 1572872 | tf_op jit(solution)/shard_map/ppermute | solution.py:242
  93.1 2.5 %collective-permute-done.31.refs_25_ = f32[2,4,64,256]{3,2,1,0:T(8,128)} collective-permute-done((f32[2,4,64,256]{3,2,1,0:T(8,128)}, f32[2,4,64,256]{3,2,1,0:T(8,128)}, u32[]{:S(2)}, u32[]{:S(2)}) %collective-permute-start.31) | collective-permute-done | bytes 524320 | tf_op jit(solution)/shard_map/ppermute | solution.py:242
  96.8 7.1 %collective-permute-done.29.refs_24_ = f32[2,4,64,256]{3,2,1,0:T(8,128)S(1)} collective-permute-done((f32[2,4,64,256]{3,2,1,0:T(8,128)}, f32[2,4,64,256]{3,2,1,0:T(8,128)S(1)}, u32[]{:S(2)}, u32[]{:S(2)}) %collective-permute-start.29) | collective-permute-done | bytes 524320 | tf_op jit(solution)/shard_map/ppermute | solution.py:242
  105.0 3.4 %collective-permute-done.12.refs_8_ = f32[2,4,64,256]{3,2,1,0:T(8,128)S(1)} collective-permute-done((f32[2,4,64,256]{3,2,1,0:T(8,128)}, f32[2,4,64,256]{3,2,1,0:T(8,128)S(1)}, u32[]{:S(2)}, u32[]{:S(2)}) %collective-permute-start.12) | collective-permute-done | bytes 524320 | tf_op jit(solution)/shard_map/ppermute | solution.py:242
  108.4 1.7 %collective-permute-start.15 = (f32[2,4,64,256]{3,2,1,0:T(8,128)S(1)}, f32[2,4,64,256]{3,2,1,0:T(8,128)S(1)}, u32[]{:S(2)}, u32[]{:S(2)}) collective-permute-start(f32[2,4,64,256]{3,2,1,0:T(8,128)S(1)} %collective-permute-done.12.refs_8_), channel_id=1, source_target_pairs={{32,0},{0,32},{40,8},{8,40},{48,16},{16,48},{56,24},{24,56},{33,1}... | collective-permute-start | bytes 1572872 | tf_op jit(solution)/shard_map/ppermute | solution.py:242
  116.9 28.6 %difference.1 = f32[12,256,256]{2,1,0:T(8,128)} custom-call(s32[108]{0:T(128)S(1)} %select_n.202.index_ref, s32[36]{0:T(128)S(1)} %reshape.507.line_ref, f32[2,4,64,256]{3,2,1,0:T(8,128)S(1)} %pad_maximum_fusion.1.refs_0_, f32[2,4,64,256]{3,2,1,0:T(8,128)S(1)} %pad_maximum_fusion.2.refs_1_, f32[2,4,64,256]{3,2,1,0:T(8,128)S(1)} %copy-done.4, ...), custom_call_target="tpu_custom_call" | custom-call | tf_op jit(solution)/shard_map/difference/pallas_call | solution.py:218
  (116 shorter events, 25.6 us)
Async XLA Ops:
  0.0 12.4 %collective-permute-start = (f32[64,512]{1,0:T(8,128)}, f32[64,512]{1,0:T(8,128)S(1)}, u32[]{:S(2)}, u32[]{:S(2)}) collective-permute-start(f32[64,512]{1,0:T(8,128)} %param.8), channel_id=1, source_target_pairs={{1,0},{33,32},{9,8},{41,40},{17,16},{49,48},{25,24},{57,56},{2,1},... | collective-permute-start | bytes 393224 | tf_op jit(solution)/shard_map/ppermute | solution.py:242
  15.8 17.0 %collective-permute-start.21 = (f32[4,64,256]{2,1,0:T(8,128)S(1)}, f32[4,64,256]{2,1,0:T(8,128)S(1)}, u32[]{:S(2)}, u32[]{:S(2)}) collective-permute-start(f32[4,64,256]{2,1,0:T(8,128)S(1)} %get-tuple-element.19), channel_id=1, source_target_pairs={{16,0},{48,32},{24,8},{56,40},{0,16},{32,48},{8,24},{40,56},{17,1}... | collective-permute-start | bytes 786440 | tf_op jit(solution)/shard_map/ppermute | solution.py:242
  19.4 13.4 %collective-permute-start.3 = (f32[4,64,256]{2,1,0:T(8,128)S(1)}, f32[4,64,256]{2,1,0:T(8,128)S(1)}, u32[]{:S(2)}, u32[]{:S(2)}) collective-permute-start(f32[4,64,256]{2,1,0:T(8,128)S(1)} %get-tuple-element.20), channel_id=1, source_target_pairs={{64,0},{96,32},{72,8},{104,40},{80,16},{112,48},{88,24},{120,56},{... | collective-permute-start | bytes 786440 | tf_op jit(solution)/shard_map/ppermute | solution.py:242
  27.7 22.5 %collective-permute-start.13 = (f32[2,4,64,256]{3,2,1,0:T(8,128)S(1)}, f32[2,4,64,256]{3,2,1,0:T(8,128)S(1)}, u32[]{:S(2)}, u32[]{:S(2)}) collective-permute-start(f32[2,4,64,256]{3,2,1,0:T(8,128)S(1)} %pad_maximum_fusion.2.refs_1_), channel_id=1, source_target_pairs={{24,0},{56,32},{0,8},{32,40},{8,16},{40,48},{16,24},{48,56},{25,1}... | collective-permute-start | bytes 1572872 | tf_op jit(solution)/shard_map/ppermute | solution.py:242
  29.4 23.7 %collective-permute-start.9 = (f32[2,4,64,256]{3,2,1,0:T(8,128)S(1)}, f32[2,4,64,256]{3,2,1,0:T(8,128)}, u32[]{:S(2)}, u32[]{:S(2)}) collective-permute-start(f32[2,4,64,256]{3,2,1,0:T(8,128)S(1)} %pad_maximum_fusion.2.refs_1_), channel_id=1, source_target_pairs={{8,0},{40,32},{16,8},{48,40},{24,16},{56,48},{0,24},{32,56},{9,1},... | collective-permute-start | bytes 1572872 | tf_op jit(solution)/shard_map/ppermute | solution.py:242
  31.6 21.5 %collective-permute-start.8 = (f32[2,4,64,256]{3,2,1,0:T(8,128)S(1)}, f32[2,4,64,256]{3,2,1,0:T(8,128)S(1)}, u32[]{:S(2)}, u32[]{:S(2)}) collective-permute-start(f32[2,4,64,256]{3,2,1,0:T(8,128)S(1)} %pad_maximum_fusion.2.refs_1_), channel_id=1, source_target_pairs={{32,0},{0,32},{40,8},{8,40},{48,16},{16,48},{56,24},{24,56},{33,1}... | collective-permute-start | bytes 1572872 | tf_op jit(solution)/shard_map/ppermute | solution.py:242
  32.8 15.7 %collective-permute-start.22 = (f32[4,64,256]{2,1,0:T(8,128)S(1)}, f32[4,64,256]{2,1,0:T(8,128)S(1)}, u32[]{:S(2)}, u32[]{:S(2)}) collective-permute-start(f32[4,64,256]{2,1,0:T(8,128)S(1)} %get-tuple-element.19), channel_id=1, source_target_pairs={{24,0},{56,32},{0,8},{32,40},{8,16},{40,48},{16,24},{48,56},{25,1}... | collective-permute-start | bytes 786440 | tf_op jit(solution)/shard_map/ppermute | solution.py:242
  32.8 15.7 %collective-permute-start.20 = (f32[4,64,256]{2,1,0:T(8,128)S(1)}, f32[4,64,256]{2,1,0:T(8,128)S(1)}, u32[]{:S(2)}, u32[]{:S(2)}) collective-permute-start(f32[4,64,256]{2,1,0:T(8,128)S(1)} %get-tuple-element.19), channel_id=1, source_target_pairs={{8,0},{40,32},{16,8},{48,40},{24,16},{56,48},{0,24},{32,56},{9,1},... | collective-permute-start | bytes 786440 | tf_op jit(solution)/shard_map/ppermute | solution.py:242
  48.5 13.3 %collective-permute-start.17 = (f32[2,4,64,256]{3,2,1,0:T(8,128)S(1)}, f32[2,4,64,256]{3,2,1,0:T(8,128)}, u32[]{:S(2)}, u32[]{:S(2)}) collective-permute-start(f32[2,4,64,256]{3,2,1,0:T(8,128)S(1)} %pad_maximum_fusion.1.refs_0_), channel_id=1, source_target_pairs={{24,0},{56,32},{0,8},{32,40},{8,16},{40,48},{16,24},{48,56},{25,1}... | collective-permute-start | bytes 1572872 | tf_op jit(solution)/shard_map/ppermute | solution.py:242
  48.5 15.6 %collective-permute-start.7 = (f32[2,4,64,256]{3,2,1,0:T(8,128)S(1)}, f32[2,4,64,256]{3,2,1,0:T(8,128)S(1)}, u32[]{:S(2)}, u32[]{:S(2)}) collective-permute-start(f32[2,4,64,256]{3,2,1,0:T(8,128)S(1)} %pad_maximum_fusion.1.refs_0_), channel_id=1, source_target_pairs={{32,0},{0,32},{40,8},{8,40},{48,16},{16,48},{56,24},{24,56},{33,1}... | collective-permute-start | bytes 1572872 | tf_op jit(solution)/shard_map/ppermute | solution.py:242
  50.1 14.8 %collective-permute-start.4 = (f32[2,4,64,256]{3,2,1,0:T(8,128)S(1)}, f32[2,4,64,256]{3,2,1,0:T(8,128)S(1)}, u32[]{:S(2)}, u32[]{:S(2)}) collective-permute-start(f32[2,4,64,256]{3,2,1,0:T(8,128)S(1)} %pad_maximum_fusion.1.refs_0_), channel_id=1, source_target_pairs={{8,0},{40,32},{16,8},{48,40},{24,16},{56,48},{0,24},{32,56},{9,1},... | collective-permute-start | bytes 1572872 | tf_op jit(solution)/shard_map/ppermute | solution.py:242
  53.1 14.5 %collective-permute-start.30 = (f32[2,4,64,256]{3,2,1,0:T(8,128)S(1)}, f32[2,4,64,256]{3,2,1,0:T(8,128)}, u32[]{:S(2)}, u32[]{:S(2)}) collective-permute-start(f32[2,4,64,256]{3,2,1,0:T(8,128)S(1)} %pad_maximum_fusion.4.refs_17_), channel_id=1, source_target_pairs={{68,0},{100,32},{76,8},{108,40},{84,16},{116,48},{92,24},{124,56},... | collective-permute-start | bytes 1572872 | tf_op jit(solution)/shard_map/ppermute | solution.py:242
  53.9 14.8 %collective-permute-start.26 = (f32[2,4,64,256]{3,2,1,0:T(8,128)S(1)}, f32[2,4,64,256]{3,2,1,0:T(8,128)S(1)}, u32[]{:S(2)}, u32[]{:S(2)}) collective-permute-start(f32[2,4,64,256]{3,2,1,0:T(8,128)S(1)} %pad_maximum_fusion.4.refs_17_), channel_id=1, source_target_pairs={{64,0},{96,32},{72,8},{104,40},{80,16},{112,48},{88,24},{120,56},{... | collective-permute-start | bytes 1572872 | tf_op jit(solution)/shard_map/ppermute | solution.py:242
  64.9 14.8 %collective-permute-start.34 = (f32[2,4,64,256]{3,2,1,0:T(8,128)S(1)}, f32[2,4,64,256]{3,2,1,0:T(8,128)}, u32[]{:S(2)}, u32[]{:S(2)}) collective-permute-start(f32[2,4,64,256]{3,2,1,0:T(8,128)S(1)} %pad_maximum_fusion.3.refs_16_), channel_id=1, source_target_pairs={{68,0},{100,32},{76,8},{108,40},{84,16},{116,48},{92,24},{124,56},... | collective-permute-start | bytes 1572872 | tf_op jit(solution)/shard_map/ppermute | solution.py:242
  64.9 15.6 %collective-permute-start.25 = (f32[2,4,64,256]{3,2,1,0:T(8,128)S(1)}, f32[2,4,64,256]{3,2,1,0:T(8,128)}, u32[]{:S(2)}, u32[]{:S(2)}) collective-permute-start(f32[2,4,64,256]{3,2,1,0:T(8,128)S(1)} %pad_maximum_fusion.3.refs_16_), channel_id=1, source_target_pairs={{64,0},{96,32},{72,8},{104,40},{80,16},{112,48},{88,24},{120,56},{... | collective-permute-start | bytes 1572872 | tf_op jit(solution)/shard_map/ppermute | solution.py:242
  67.6 13.0 %collective-permute-start.23 = (f32[2,4,64,256]{3,2,1,0:T(8,128)S(1)}, f32[2,4,64,256]{3,2,1,0:T(8,128)}, u32[]{:S(2)}, u32[]{:S(2)}) collective-permute-start(f32[2,4,64,256]{3,2,1,0:T(8,128)S(1)} %pad_maximum_fusion.3.refs_16_), channel_id=1, source_target_pairs={{32,0},{0,32},{40,8},{8,40},{48,16},{16,48},{56,24},{24,56},{33,1}... | collective-permute-start | bytes 1572872 | tf_op jit(solution)/shard_map/ppermute | solution.py:242
  70.6 18.8 %collective-permute-start.14 = (f32[2,4,64,256]{3,2,1,0:T(8,128)S(1)}, f32[2,4,64,256]{3,2,1,0:T(8,128)}, u32[]{:S(2)}, u32[]{:S(2)}) collective-permute-start(f32[2,4,64,256]{3,2,1,0:T(8,128)S(1)} %collective-permute-done.13.refs_13_), channel_id=1, source_target_pairs={{24,0},{56,32},{0,8},{32,40},{8,16},{40,48},{16,24},{48,56},{25,1}... | collective-permute-start | bytes 1572872 | tf_op jit(solution)/shard_map/ppermute | solution.py:242
  79.7 12.8 %collective-permute-start.36 = (f32[2,4,64,256]{3,2,1,0:T(8,128)}, f32[2,4,64,256]{3,2,1,0:T(8,128)}, u32[]{:S(2)}, u32[]{:S(2)}) collective-permute-start(f32[2,4,64,256]{3,2,1,0:T(8,128)} %collective-permute-done.30.refs_29_), channel_id=1, source_target_pairs={{32,0},{0,32},{40,8},{8,40},{48,16},{16,48},{56,24},{24,56},{33,1}... | collective-permute-start | bytes 1572872 | tf_op jit(solution)/shard_map/ppermute | solution.py:242
  80.6 15.0 %collective-permute-start.31 = (f32[2,4,64,256]{3,2,1,0:T(8,128)}, f32[2,4,64,256]{3,2,1,0:T(8,128)}, u32[]{:S(2)}, u32[]{:S(2)}) collective-permute-start(f32[2,4,64,256]{3,2,1,0:T(8,128)} %collective-permute-done.30.refs_29_), channel_id=1, source_target_pairs={{68,0},{100,32},{76,8},{108,40},{84,16},{116,48},{92,24},{124,56},... | collective-permute-start | bytes 1572872 | tf_op jit(solution)/shard_map/ppermute | solution.py:242
  89.9 14.0 %collective-permute-start.29 = (f32[2,4,64,256]{3,2,1,0:T(8,128)}, f32[2,4,64,256]{3,2,1,0:T(8,128)S(1)}, u32[]{:S(2)}, u32[]{:S(2)}) collective-permute-start(f32[2,4,64,256]{3,2,1,0:T(8,128)} %collective-permute-done.25.refs_20_), channel_id=1, source_target_pairs={{64,0},{96,32},{72,8},{104,40},{80,16},{112,48},{88,24},{120,56},{... | collective-permute-start | bytes 1572872 | tf_op jit(solution)/shard_map/ppermute | solution.py:242
  92.5 12.5 %collective-permute-start.27 = (f32[2,4,64,256]{3,2,1,0:T(8,128)}, f32[2,4,64,256]{3,2,1,0:T(8,128)S(1)}, u32[]{:S(2)}, u32[]{:S(2)}) collective-permute-start(f32[2,4,64,256]{3,2,1,0:T(8,128)} %collective-permute-done.25.refs_20_), channel_id=1, source_target_pairs={{32,0},{0,32},{40,8},{8,40},{48,16},{16,48},{56,24},{24,56},{33,1}... | collective-permute-start | bytes 1572872 | tf_op jit(solution)/shard_map/ppermute | solution.py:242
  95.6 12.8 %collective-permute-start.12 = (f32[2,4,64,256]{3,2,1,0:T(8,128)}, f32[2,4,64,256]{3,2,1,0:T(8,128)S(1)}, u32[]{:S(2)}, u32[]{:S(2)}) collective-permute-start(f32[2,4,64,256]{3,2,1,0:T(8,128)} %copy-done.5), channel_id=1, source_target_pairs={{8,0},{40,32},{16,8},{48,40},{24,16},{56,48},{0,24},{32,56},{9,1},... | collective-permute-start | bytes 1572872 | tf_op jit(solution)/shard_map/ppermute | solution.py:242
  95.6 14.5 %collective-permute-start.10 = (f32[2,4,64,256]{3,2,1,0:T(8,128)}, f32[2,4,64,256]{3,2,1,0:T(8,128)S(1)}, u32[]{:S(2)}, u32[]{:S(2)}) collective-permute-start(f32[2,4,64,256]{3,2,1,0:T(8,128)} %copy-done.5), channel_id=1, source_target_pairs={{32,0},{0,32},{40,8},{8,40},{48,16},{16,48},{56,24},{24,56},{33,1}... | collective-permute-start | bytes 1572872 | tf_op jit(solution)/shard_map/ppermute | solution.py:242
  96.7 13.4 %collective-permute-start.16 = (f32[2,4,64,256]{3,2,1,0:T(8,128)}, f32[2,4,64,256]{3,2,1,0:T(8,128)S(1)}, u32[]{:S(2)}, u32[]{:S(2)}) collective-permute-start(f32[2,4,64,256]{3,2,1,0:T(8,128)} %collective-permute-done.14.refs_9_), channel_id=1, source_target_pairs={{32,0},{0,32},{40,8},{8,40},{48,16},{16,48},{56,24},{24,56},{33,1}... | collective-permute-start | bytes 1572872 | tf_op jit(solution)/shard_map/ppermute | solution.py:242
  (28 other events, 324.9 us)
